TPU v7x, 128 devices: a whole 4x4x4 slice. The times are simulated.
128 devices in a mesh: dp: 8 (over z_hi, y), fsdp: 16 (over z_lo, x, core).
Axes of the slice: x: 4, y: 4, z: 4 (z_hi: 2, z_lo: 2; z = z_hi * 2 + z_lo), core: 2. Of those that a mesh axis runs over, the one named last changes fastest.
Arguments:
- weight: float32 [4096, 15360], P('fsdp', 'dp'), may hold values from -0.09375 to 0.09375
- history: float32 [7, 4096, 15360], P(None, 'fsdp', 'dp'), may hold values from -6 to 6
- newest: int32 [1], replicated, may hold values from 0 to 6
- band: float32 [8], replicated, may hold values from 0.5 to 1.5
- fresh: bfloat16 [4096, 15360], P('fsdp', 'dp'), may hold values from -6 to 6
- x_grad: bfloat16 [1024, 4096], P('dp', 'fsdp'), may hold values from -96 to 96
- dy_grad: bfloat16 [1024, 15360], P('dp'), may hold values from -6 to 6
- x_next: bfloat16 [6144, 4096], P('fsdp'), may hold values from -6 to 6
Outputs:
- new_weight: float32 [4096, 15360], P('fsdp', 'dp')
- noise_now: float32 [4096, 15360], P('fsdp', 'dp')
- next_out: bfloat16 [6144, 15360], P('fsdp', 'dp')
All inputs are finite; a program needn't handle non-finite values.
Results may differ from a plain program's by a relative error of at most 0.005.
Values may be sent and summed in bfloat16 or wider, within the bound.
A program may use at most 128 MiB of HBM per device.

v0:
```python
import math
import jax
import jax.numpy as jnp
from jax import lax
from jax.sharding import PartitionSpec as P

eps_value = 1e-06
learn_rate = 0.2
noise_multiplier = 0.01


def slot_weights(newest, band, slots):
    slot_index = jnp.arange(slots, dtype=jnp.int32)
    ages = (newest[0] - slot_index) % slots + 1
    table_index = jnp.arange(slots + 1, dtype=jnp.int32)
    return jnp.sum(jnp.where(ages[:, None] == table_index[None, :], band[None, :], 0.0), axis=1)


def local(weight, history, newest, band, fresh, x_grad, dy_grad, x_next):
    full_width = x_next.shape[1]
    hidden_units = dy_grad.shape[1]
    clip_bound = 2.0 * math.sqrt(full_width * hidden_units)
    dy_mine = lax.all_to_all(dy_grad, "dp", split_axis=1, concat_axis=0, tiled=True)
    x_float = x_grad.astype(jnp.float32)
    feature_sq = lax.psum(jnp.sum(x_float * x_float, axis=1), "fsdp")
    output_sq = jnp.sum(jnp.square(dy_grad.astype(jnp.float32)), axis=1)
    factor = jnp.minimum(1.0, clip_bound / jnp.sqrt(feature_sq * output_sq + eps_value))
    clipped = (factor[:, None] * x_float).astype(jnp.bfloat16)
    clipped_all = lax.all_gather(clipped, "dp", axis=0, tiled=True)
    contract = (((0,), (0,)), ((), ()))
    gradient = lax.dot_general(clipped_all, dy_mine, contract, preferred_element_type=jnp.float32)
    tokens_all = x_grad.shape[0] * lax.axis_size("dp")
    slots = history.shape[0]
    mixing = slot_weights(newest, band, slots)
    combined = jnp.tensordot(mixing, history, axes=1, precision=lax.Precision.HIGHEST)
    noise_now = (fresh.astype(jnp.float32) - combined) / band[0]
    new_weight = (
        weight - learn_rate * (gradient + noise_multiplier * clip_bound * noise_now) / tokens_all
    )
    weight_half = new_weight.astype(jnp.bfloat16)
    next_float = jnp.dot(
        x_next,
        lax.all_gather(weight_half, "fsdp", axis=0, tiled=True),
        preferred_element_type=jnp.float32,
    )
    return (new_weight, noise_now, next_float.astype(jnp.bfloat16))


def solution(mesh):
    in_specs = (
        P("fsdp", "dp"),
        P(None, "fsdp", "dp"),
        P(),
        P(),
        P("fsdp", "dp"),
        P("dp", "fsdp"),
        P("dp", None),
        P("fsdp", None),
    )
    out_specs = (P("fsdp", "dp"), P("fsdp", "dp"), P("fsdp", "dp"))
    return jax.shard_map(local, mesh=mesh, in_specs=in_specs, out_specs=out_specs, check_vma=False)
```

profile of v0, /device:TPU:1, one launch (start us, length us, event | category | flops | bytes accessed | tf_op | source)
XLA Modules:
  0.0 260.5 jit_solution(6377903200026531716)
XLA Ops:
  7.2 0.0 copy-start
  7.2 6.4 %copy.16 = bf16[128,15360]{0,1:T(8,128)(2,1)} copy(bf16[128,15360]{1,0:T(8,128)(2,1)} %param.14) | data formatting | bytes 7864320 | tf_op args[6]
  13.6 0.0 copy-start.2
  13.6 8.5 %all-to-all-start = ((bf16[128,8,1920]{0,2,1:T(8,128)(2,1)}), bf16[128,8,1920]{0,2,1:T(8,128)(2,1)}, u32[]{:S(2)}, u32[]{:S(2)}) async-start(bf16[128,8,1920]{0,2,1:T(8,128)(2,1)} %bitcast.20), calls=%async_computation | async-start | bytes 7864320 | tf_op jit(solution)/shard_map/all_to_all | solution.py:23
  22.0 0.0 all-gather.2.cloned.1.call-start
  22.7 0.0 copy-done.2
  22.7 0.1 fusion.6
  22.9 33.2 %psum.7 = f32[128]{0:T(128)S(1)} all-reduce(f32[128]{0:T(128)S(1)} %fusion.6), channel_id=1, replica_groups=mesh['dp'=8,'fsdp'=16] {'fsdp'}, use_global_device_ids=true, to_apply=%region_1.0 | all-reduce | flops 128 | bytes 1024 | tf_op jit(solution)/shard_map/psum | solution.py:25
  56.1 0.0 copy-done.3
  56.1 0.2 select_reduce_fusion
  56.3 3.0 %multiply_reduce_fusion = f32[128]{0:T(128)S(1)} fusion(bf16[128,15360]{1,0:T(8,128)(2,1)} %param.14), kind=kLoop, calls=%fused_computation.2 | loop fusion | flops 5898112 | bytes 3932672 | tf_op jit(solution)/shard_map/reduce_sum | solution.py:26
  59.3 0.1 fusion.7
  59.4 44.9 %all_gather.6 = bf16[1024,256]{1,0:T(8,128)(2,1)} all-gather(bf16[128,256]{1,0:T(8,128)(2,1)S(1)} %fusion.7), channel_id=1, replica_groups=mesh['dp'=8,'fsdp'=16] {'dp'}, dimensions={0}, use_global_device_ids=true | all-gather | bytes 589824 | tf_op jit(solution)/shard_map/all_gather | solution.py:29
  104.2 26.8 %fusion = f32[1,256,1920]{2,0,1:T(1,128)S(1)} fusion(f32[7,256,1920]{2,1,0:T(8,128)} %param.9, f32[7]{0:T(128)S(1)} %select_reduce_fusion), kind=kOutput, calls=%fused_computation | convolution fusion | flops 41287680 | bytes 15728668 | tf_op jit(solution)/shard_map/dot_general | solution.py:35
  131.1 0.0 copy-done.1
  131.1 1.5 fusion.5
  132.6 0.0 all-to-all-done
  132.6 6.4 %copy.17 = bf16[8,128,1920]{2,1,0:T(8,128)(2,1)} copy(bf16[8,128,1920]{1,2,0:T(8,128)(2,1)} %bitcast.1) | data formatting | bytes 7864320 | tf_op jit(solution)/shard_map/all_to_all | solution.py:23
  139.0 6.4 %fusion.10 = (bf16[256,1920]{1,0:T(8,128)(2,1)}, f32[256,1920]{1,0:T(8,128)}) fusion(f32[256,1920]{1,0:T(8,128)} %param.8, f32[256,1920]{1,0:T(8,128)} %fusion.5, bf16[1024,256]{1,0:T(8,128)(2,1)} %all_gather.6, bf16[1024,1920]{1,0:T(8,128)(2,1)} %bitcast.21), kind=kOutput, calls=%fused_computation.20 | convolution fusion | flops 1009090560 | bytes 11337728 | tf_op jit(solution)/shard_map/dot_general | solution.py:31
  145.4 0.0 all-gather.2.cloned.1.call-update
  145.4 92.6 %all-gather.2.cloned.1.call-done = bf16[4096,1920]{1,0:T(8,128)(2,1)} async-done(((bf16[256,1920]{1,0:T(8,128)(2,1)}), bf16[4096,1920]{1,0:T(8,128)(2,1)}) %all-gather.2.cloned.1.call-update) | async-done | bytes 15728656 | tf_op jit(solution)/shard_map/all_gather | solution.py:43
  238.0 0.0 copy-done
  238.0 13.1 %fusion.4 = bf16[384,1920]{0,1:T(8,128)(2,1)} fusion(bf16[4096,1920]{1,0:T(8,128)(2,1)} %all-gather.2.cloned.1.call-done, bf16[384,4096]{1,0:T(8,128)(2,1)S(1)} %copy-done), kind=kOutput, calls=%fused_computation.7 | convolution fusion | flops 6040535040 | bytes 20348928 | tf_op jit(solution)/shard_map/dot_general | solution.py:41
  251.1 2.5 copy.18
  (4 shorter events, 0.0 us)
Async XLA Ops:
  7.2 230.8 %copy-start = (bf16[384,4096]{1,0:T(8,128)(2,1)S(1)}, bf16[384,4096]{1,0:T(8,128)(2,1)}, u32[]{:S(2)}) copy-start(bf16[384,4096]{1,0:T(8,128)(2,1)} %param.15) | copy-start | bytes 9437188
  13.6 9.2 %copy-start.2 = (bf16[128,256]{1,0:T(8,128)(2,1)S(1)}, bf16[128,256]{1,0:T(8,128)(2,1)}, u32[]{:S(2)}) copy-start(bf16[128,256]{1,0:T(8,128)(2,1)} %param.13) | copy-start | bytes 196612
  13.6 42.5 %copy-start.3 = (f32[8]{0:T(128)S(1)}, f32[8]{0:T(128)}, u32[]{:S(2)}) copy-start(f32[8]{0:T(128)} %param.11) | copy-start | bytes 100
  13.6 119.0 %all-to-all-start = ((bf16[128,8,1920]{0,2,1:T(8,128)(2,1)}), bf16[128,8,1920]{0,2,1:T(8,128)(2,1)}, u32[]{:S(2)}, u32[]{:S(2)}) async-start(bf16[128,8,1920]{0,2,1:T(8,128)(2,1)} %bitcast.20), calls=%async_computation | async-start | bytes 7864320 | tf_op jit(solution)/shard_map/all_to_all | solution.py:23
  22.0 215.9 %all-gather.2.cloned.1.call-start = ((), (), s32[]{:S(2)}) async-start(), calls=%async_computation.1 | async-start | bytes 16711680 | tf_op jit(solution)/shard_map/all_gather | solution.py:43
  104.2 26.8 %copy-start.1 = (bf16[256,1920]{1,0:T(8,128)(2,1)S(1)}, bf16[256,1920]{1,0:T(8,128)(2,1)}, u32[]{:S(2)}) copy-start(bf16[256,1920]{1,0:T(8,128)(2,1)} %param.12) | copy-start | bytes 2949124
Sparse Core Ops, SparseCore 0:
  145.5 92.3 all-gather.1
where the time goes:
time: 261 us; the launch traced here: 260 us
  waiting for transfers between devices  92.6 us (35%)
  blocking collectives  78.1 us (30%)
  matrix products  46.4 us (18%)
  local copies, waits for them, and re-layouts  15.4 us (6%)
  between operations  14.7 us (6%)
  starting transfers between devices  8.49 us (3%)
  other arithmetic  4.86 us (2%)
    all_gather x1, waiting for transfers between devices, local(): lax.all_gather(weight_half, 'fsdp', axis=0, tiled=True)  92.6 us
    all_gather x1, blocking collectives, local(): clipped_all = lax.all_gather(clipped, 'dp', axis=0, tiled=True)  44.9 us
    psum x1, blocking collectives, local(): feature_sq = lax.psum(jnp.sum(x_float * x_float, axis=1), 'fsdp')  33.2 us
    dot_general x1, matrix products, local(): jnp.tensordot(mixing, history, axes=1, precision=lax.Precision.HIGHEST)  26.8 us
    dot_general x1, matrix products, local(): jnp.dot(x_next, lax.all_gather(weight_half, 'fsdp', axis=0, tiled=True),...  13.1 us
    unnamed x10, local copies, waits for them, and re-layouts  8.98 us
    all_to_all x1, starting transfers between devices, local(): lax.all_to_all(dy_grad, 'dp', split_axis=1, concat_axis=0, tiled=True)  8.45 us
    dot_general x1, matrix products, local(): lax.dot_general(clipped_all, dy_mine, contract, preferred_element_type=jn...  6.44 us
  transfers between devices with their start and end apart: 2, of which 1 were waited for; matrix products, arithmetic and copies ran while one was open for 12% of the time, Pallas kernels for 0%

commit v1 on v0

--- a/solution.py
+++ b/solution.py
@@ -40,7 +40,9 @@
     weight_half = new_weight.astype(jnp.bfloat16)
     next_float = jnp.dot(
         x_next,
-        lax.all_gather(weight_half, "fsdp", axis=0, tiled=True),
+        jnp.concatenate(
+            lax.all_to_all(jnp.stack([weight_half] * lax.axis_size("fsdp")), "fsdp", 0, 0), axis=0
+        ),
         preferred_element_type=jnp.float32,
     )
     return (new_weight, noise_now, next_float.astype(jnp.bfloat16))

time: 261 us -> 337 us (1.29)
  blocking collectives: 78.1 us -> 261 us
  waiting for transfers between devices: 92.6 us -> 0.01 us
  between operations: 14.7 us -> 1.35 us
  matrix products: 46.4 us -> 42.7 us
    all_to_all x0 -> x1, blocking collectives: none -> 183 us  [local(): lax.all_to_all(jnp.stack([weight_half] * lax.axis_size('fsdp')), 'fsdp',...]
    all_gather x1 -> x0, waiting for transfers between devices: 92.6 us -> none  [local(): lax.all_gather(weight_half, 'fsdp', axis=0, tiled=True)]
    dot_general x1, matrix products: 13.1 us -> 9.72 us  [local(): jnp.dot(x_next, jnp.concatenate(lax.all_to_all(jnp.stack([weight_half] *...]
  transfers between devices with their start and end apart: 2 -> 1, of which waited for: 1 -> 0; matrix products, arithmetic and copies ran while one was open for 12% -> 9% of each run, Pallas kernels for 0% -> 0%
where the time goes in v1:
time: 337 us; the launch traced here: 336 us
  blocking collectives  261 us (77%)
  matrix products  42.7 us (13%)
  local copies, waits for them, and re-layouts  17.4 us (5%)
  starting transfers between devices  8.45 us (3%)
  other arithmetic  4.86 us (1%)
    all_to_all x1, blocking collectives, local(): lax.all_to_all(jnp.stack([weight_half] * lax.axis_size('fsdp')), 'fsdp',...  183 us
    all_gather x1, blocking collectives, local(): clipped_all = lax.all_gather(clipped, 'dp', axis=0, tiled=True)  44.9 us
    psum x1, blocking collectives, local(): feature_sq = lax.psum(jnp.sum(x_float * x_float, axis=1), 'fsdp')  33.2 us
    dot_general x1, matrix products, local(): jnp.tensordot(mixing, history, axes=1, precision=lax.Precision.HIGHEST)  26.8 us
    dot_general x1, matrix products, local(): jnp.dot(x_next, jnp.concatenate(lax.all_to_all(jnp.stack([weight_half] *...  9.72 us
    unnamed x10, local copies, waits for them, and re-layouts  8.98 us
    all_to_all x1, starting transfers between devices, local(): lax.all_to_all(dy_grad, 'dp', split_axis=1, concat_axis=0, tiled=True)  8.45 us
  transfers between devices with their start and end apart: 1, of which 0 were waited for; matrix products, arithmetic and copies ran while one was open for 9% of the time, Pallas kernels for 0%

profile of v1, /device:TPU:1, one launch (start us, length us, event | category | flops | bytes accessed | tf_op | source)
XLA Modules:
  0.0 336.2 jit_solution(1325512233760579883)
XLA Ops:
  0.6 0.0 copy-start
  0.6 6.4 %copy.16 = bf16[128,15360]{0,1:T(8,128)(2,1)} copy(bf16[128,15360]{1,0:T(8,128)(2,1)} %param.14) | data formatting | bytes 7864320 | tf_op args[6]
  7.1 0.0 copy-start.2
  7.1 0.0 copy-start.3
  7.1 8.5 %all-to-all-start = ((bf16[128,8,1920]{0,2,1:T(8,128)(2,1)}), bf16[128,8,1920]{0,2,1:T(8,128)(2,1)}, u32[]{:S(2)}, u32[]{:S(2)}) async-start(bf16[128,8,1920]{0,2,1:T(8,128)(2,1)} %bitcast.22), calls=%async_computation | async-start | bytes 7864320 | tf_op jit(solution)/shard_map/all_to_all | solution.py:23
  16.2 0.0 copy-done.2
  16.2 0.1 fusion.6
  16.3 33.2 %psum.7 = f32[128]{0:T(128)S(1)} all-reduce(f32[128]{0:T(128)S(1)} %fusion.6), channel_id=1, replica_groups=mesh['dp'=8,'fsdp'=16] {'fsdp'}, use_global_device_ids=true, to_apply=%region_1.0 | all-reduce | flops 128 | bytes 1024 | tf_op jit(solution)/shard_map/psum | solution.py:25
  49.5 0.0 copy-done.3
  49.6 0.2 select_reduce_fusion
  49.7 3.0 multiply_reduce_fusion
  52.7 0.1 fusion.7
  52.8 44.9 %all_gather.3 = bf16[1024,256]{1,0:T(8,128)(2,1)} all-gather(bf16[128,256]{1,0:T(8,128)(2,1)S(1)} %fusion.7), channel_id=1, replica_groups=mesh['dp'=8,'fsdp'=16] {'dp'}, dimensions={0}, use_global_device_ids=true | all-gather | bytes 589824 | tf_op jit(solution)/shard_map/all_gather | solution.py:29
  97.7 26.8 %fusion = f32[1,256,1920]{2,0,1:T(1,128)S(1)} fusion(f32[7,256,1920]{2,1,0:T(8,128)} %param.9, f32[7]{0:T(128)S(1)} %select_reduce_fusion), kind=kOutput, calls=%fused_computation | convolution fusion | flops 41287680 | bytes 15728668 | tf_op jit(solution)/shard_map/dot_general | solution.py:35
  124.5 0.0 copy-done.1
  124.5 1.5 fusion.5
  126.0 0.0 all-to-all-done
  126.0 6.4 %copy.17 = bf16[8,128,1920]{2,1,0:T(8,128)(2,1)} copy(bf16[8,128,1920]{1,2,0:T(8,128)(2,1)} %bitcast.1) | data formatting | bytes 7864320 | tf_op jit(solution)/shard_map/all_to_all | solution.py:23
  132.4 6.1 %fusion.10 = (bf16[256,1920]{1,0:T(8,128)(2,1)S(1)}, f32[256,1920]{1,0:T(8,128)}) fusion(f32[256,1920]{1,0:T(8,128)} %param.8, f32[256,1920]{1,0:T(8,128)} %fusion.5, bf16[1024,256]{1,0:T(8,128)(2,1)} %all_gather.3, bf16[1024,1920]{1,0:T(8,128)(2,1)} %bitcast.23), kind=kOutput, calls=%fused_computation.20 | convolution fusion | flops 1009090560 | bytes 11337728 | tf_op jit(solution)/shard_map/dot_general | solution.py:31
  138.5 2.0 stack.2
  140.6 183.3 %all_to_all.24 = bf16[16,256,1920]{2,1,0:T(8,128)(2,1)S(1)} all-to-all(bf16[16,256,1920]{2,1,0:T(8,128)(2,1)S(1)} %stack.2), channel_id=1, replica_groups=mesh['dp'=8,'fsdp'=16] {'fsdp'}, dimensions={0} | all-to-all | bytes 31457280 | tf_op jit(solution)/shard_map/all_to_all | solution.py:44
  323.9 0.0 copy-done
  323.9 9.7 %fusion.4 = bf16[384,1920]{0,1:T(8,128)(2,1)} fusion(bf16[4096,1920]{1,0:T(8,128)(2,1)S(1)} %bitcast.21, bf16[384,4096]{1,0:T(8,128)(2,1)S(1)} %copy-done), kind=kOutput, calls=%fused_computation.7 | convolution fusion | flops 6040535040 | bytes 20348928 | tf_op jit(solution)/shard_map/dot_general | solution.py:41
  333.6 2.5 copy.18
  (3 shorter events, 0.0 us)
Async XLA Ops:
  0.6 323.2 %copy-start = (bf16[384,4096]{1,0:T(8,128)(2,1)S(1)}, bf16[384,4096]{1,0:T(8,128)(2,1)}, u32[]{:S(2)}) copy-start(bf16[384,4096]{1,0:T(8,128)(2,1)} %param.15) | copy-start | bytes 9437188
  7.1 9.1 %copy-start.2 = (bf16[128,256]{1,0:T(8,128)(2,1)S(1)}, bf16[128,256]{1,0:T(8,128)(2,1)}, u32[]{:S(2)}) copy-start(bf16[128,256]{1,0:T(8,128)(2,1)} %param.13) | copy-start | bytes 196612
  7.1 42.5 %copy-start.3 = (f32[8]{0:T(128)S(1)}, f32[8]{0:T(128)}, u32[]{:S(2)}) copy-start(f32[8]{0:T(128)} %param.11) | copy-start | bytes 100
  7.1 119.0 %all-to-all-start = ((bf16[128,8,1920]{0,2,1:T(8,128)(2,1)}), bf16[128,8,1920]{0,2,1:T(8,128)(2,1)}, u32[]{:S(2)}, u32[]{:S(2)}) async-start(bf16[128,8,1920]{0,2,1:T(8,128)(2,1)} %bitcast.22), calls=%async_computation | async-start | bytes 7864320 | tf_op jit(solution)/shard_map/all_to_all | solution.py:23
  97.7 26.8 %copy-start.1 = (bf16[256,1920]{1,0:T(8,128)(2,1)S(1)}, bf16[256,1920]{1,0:T(8,128)(2,1)}, u32[]{:S(2)}) copy-start(bf16[256,1920]{1,0:T(8,128)(2,1)} %param.12) | copy-start | bytes 2949124

commit v2 on v0

--- a/solution.py
+++ b/solution.py
@@ -22,7 +22,7 @@
     clip_bound = 2.0 * math.sqrt(full_width * hidden_units)
     dy_mine = lax.all_to_all(dy_grad, "dp", split_axis=1, concat_axis=0, tiled=True)
     x_float = x_grad.astype(jnp.float32)
-    feature_sq = lax.psum(jnp.sum(x_float * x_float, axis=1), "fsdp")
+    feature_sq = jnp.sum(lax.all_gather(jnp.sum(x_float * x_float, axis=1), "fsdp"), axis=0)
     output_sq = jnp.sum(jnp.square(dy_grad.astype(jnp.float32)), axis=1)
     factor = jnp.minimum(1.0, clip_bound / jnp.sqrt(feature_sq * output_sq + eps_value))
     clipped = (factor[:, None] * x_float).astype(jnp.bfloat16)

time: 261 us -> 260 us (level)
    psum x1 -> x0, blocking collectives: 33.2 us -> none  [local(): feature_sq = lax.psum(jnp.sum(x_float * x_float, axis=1), 'fsdp')]
    all_gather x0 -> x1, blocking collectives: none -> 21.7 us  [local(): lax.all_gather(jnp.sum(x_float * x_float, axis=1), 'fsdp')]
    all_gather x1, blocking collectives: 44.9 us -> 55.7 us  [local(): clipped_all = lax.all_gather(clipped, 'dp', axis=0, tiled=True)]
where the time goes in v2:
time: 260 us
  waiting for transfers between devices  92.2 us (35%)
  blocking collectives  77.4 us (30%)
  matrix products  46.4 us (18%)
  local copies, waits for them, and re-layouts  15.4 us (6%)
  between operations  14.7 us (6%)
  starting transfers between devices  8.49 us (3%)
  other arithmetic  4.9 us (2%)
    all_gather x1, waiting for transfers between devices, local(): lax.all_gather(weight_half, 'fsdp', axis=0, tiled=True)  92.2 us
    all_gather x1, blocking collectives, local(): clipped_all = lax.all_gather(clipped, 'dp', axis=0, tiled=True)  55.7 us
    dot_general x1, matrix products, local(): jnp.tensordot(mixing, history, axes=1, precision=lax.Precision.HIGHEST)  26.8 us
    all_gather x1, blocking collectives, local(): lax.all_gather(jnp.sum(x_float * x_float, axis=1), 'fsdp')  21.7 us
    dot_general x1, matrix products, local(): jnp.dot(x_next, lax.all_gather(weight_half, 'fsdp', axis=0, tiled=True),...  13.1 us
    unnamed x10, local copies, waits for them, and re-layouts  8.98 us
    all_to_all x1, starting transfers between devices, local(): lax.all_to_all(dy_grad, 'dp', split_axis=1, concat_axis=0, tiled=True)  8.45 us
    dot_general x1, matrix products, local(): lax.dot_general(clipped_all, dy_mine, contract, preferred_element_type=jn...  6.44 us
  transfers between devices with their start and end apart: 2, of which 1 were waited for; matrix products, arithmetic and copies ran while one was open for 12% of the time, Pallas kernels for 0%

profile of v2, /device:TPU:1, one launch (start us, length us, event | category | flops | bytes accessed | tf_op | source)
XLA Modules:
  0.0 259.5 jit_solution(17001466251793879837)
XLA Ops:
  7.2 0.0 copy-start
  7.2 6.4 %copy.19 = bf16[128,15360]{0,1:T(8,128)(2,1)} copy(bf16[128,15360]{1,0:T(8,128)(2,1)} %param.14) | data formatting | bytes 7864320 | tf_op args[6]
  13.6 0.0 copy-start.2
  13.6 8.5 %all-to-all-start = ((bf16[128,8,1920]{0,2,1:T(8,128)(2,1)}), bf16[128,8,1920]{0,2,1:T(8,128)(2,1)}, u32[]{:S(2)}, u32[]{:S(2)}) async-start(bf16[128,8,1920]{0,2,1:T(8,128)(2,1)} %bitcast.21), calls=%async_computation | async-start | bytes 7864320 | tf_op jit(solution)/shard_map/all_to_all | solution.py:23
  22.0 0.0 all-gather.4.cloned.1.call-start
  22.7 0.0 copy-done.2
  22.7 0.1 fusion.6
  22.9 21.7 %all-gather.1 = f32[16,1,128]{2,1,0:T(1,128)S(1)} all-gather(f32[1,1,128]{2,1,0:T(1,128)S(1)} %bitcast.23), channel_id=2, replica_groups=mesh['dp'=8,'fsdp'=16] {'fsdp'}, dimensions={0}, use_global_device_ids=true | all-gather | bytes 8704 | tf_op jit(solution)/shard_map/all_gather | solution.py:25
  44.6 0.0 copy-done.3
  44.6 0.2 select_reduce_fusion
  44.8 3.0 %multiply_reduce_fusion = f32[128]{0:T(128)S(1)} fusion(bf16[128,15360]{1,0:T(8,128)(2,1)} %param.14), kind=kLoop, calls=%fused_computation.2 | loop fusion | flops 5898112 | bytes 3932672 | tf_op jit(solution)/shard_map/reduce_sum | solution.py:26
  47.7 0.1 fusion.7
  47.9 55.7 %all_gather.14 = bf16[1024,256]{1,0:T(8,128)(2,1)} all-gather(bf16[128,256]{1,0:T(8,128)(2,1)S(1)} %fusion.7), channel_id=1, replica_groups=mesh['dp'=8,'fsdp'=16] {'dp'}, dimensions={0}, use_global_device_ids=true | all-gather | bytes 589824 | tf_op jit(solution)/shard_map/all_gather | solution.py:29
  103.6 26.8 %fusion = f32[1,256,1920]{2,0,1:T(1,128)S(1)} fusion(f32[7,256,1920]{2,1,0:T(8,128)} %param.9, f32[7]{0:T(128)S(1)} %select_reduce_fusion), kind=kOutput, calls=%fused_computation | convolution fusion | flops 41287680 | bytes 15728668 | tf_op jit(solution)/shard_map/dot_general | solution.py:35
  130.4 0.0 copy-done.1
  130.5 1.5 fusion.5
  132.0 0.0 all-to-all-done
  132.0 6.4 %copy.20 = bf16[8,128,1920]{2,1,0:T(8,128)(2,1)} copy(bf16[8,128,1920]{1,2,0:T(8,128)(2,1)} %bitcast.2) | data formatting | bytes 7864320 | tf_op jit(solution)/shard_map/all_to_all | solution.py:23
  138.3 6.4 %fusion.10 = (bf16[256,1920]{1,0:T(8,128)(2,1)}, f32[256,1920]{1,0:T(8,128)}) fusion(f32[256,1920]{1,0:T(8,128)} %param.8, f32[256,1920]{1,0:T(8,128)} %fusion.5, bf16[1024,256]{1,0:T(8,128)(2,1)} %all_gather.14, bf16[1024,1920]{1,0:T(8,128)(2,1)} %bitcast.22), kind=kOutput, calls=%fused_computation.20 | convolution fusion | flops 1009090560 | bytes 11337728 | tf_op jit(solution)/shard_map/dot_general | solution.py:31
  144.8 0.0 all-gather.4.cloned.1.call-update
  144.8 92.2 %all-gather.4.cloned.1.call-done = bf16[4096,1920]{1,0:T(8,128)(2,1)} async-done(((bf16[256,1920]{1,0:T(8,128)(2,1)}), bf16[4096,1920]{1,0:T(8,128)(2,1)}) %all-gather.4.cloned.1.call-update) | async-done | bytes 15728656 | tf_op jit(solution)/shard_map/all_gather | solution.py:43
  237.0 0.0 copy-done
  237.0 13.1 %fusion.4 = bf16[384,1920]{0,1:T(8,128)(2,1)} fusion(bf16[4096,1920]{1,0:T(8,128)(2,1)} %all-gather.4.cloned.1.call-done, bf16[384,4096]{1,0:T(8,128)(2,1)S(1)} %copy-done), kind=kOutput, calls=%fused_computation.7 | convolution fusion | flops 6040535040 | bytes 20348928 | tf_op jit(solution)/shard_map/dot_general | solution.py:41
  250.1 2.5 copy.21
  (5 shorter events, 0.1 us)
Async XLA Ops:
  7.2 229.9 %copy-start = (bf16[384,4096]{1,0:T(8,128)(2,1)S(1)}, bf16[384,4096]{1,0:T(8,128)(2,1)}, u32[]{:S(2)}) copy-start(bf16[384,4096]{1,0:T(8,128)(2,1)} %param.15) | copy-start | bytes 9437188
  13.6 9.2 %copy-start.2 = (bf16[128,256]{1,0:T(8,128)(2,1)S(1)}, bf16[128,256]{1,0:T(8,128)(2,1)}, u32[]{:S(2)}) copy-start(bf16[128,256]{1,0:T(8,128)(2,1)} %param.13) | copy-start | bytes 196612
  13.6 31.0 %copy-start.3 = (f32[8]{0:T(128)S(1)}, f32[8]{0:T(128)}, u32[]{:S(2)}) copy-start(f32[8]{0:T(128)} %param.11) | copy-start | bytes 100
  13.6 118.4 %all-to-all-start = ((bf16[128,8,1920]{0,2,1:T(8,128)(2,1)}), bf16[128,8,1920]{0,2,1:T(8,128)(2,1)}, u32[]{:S(2)}, u32[]{:S(2)}) async-start(bf16[128,8,1920]{0,2,1:T(8,128)(2,1)} %bitcast.21), calls=%async_computation | async-start | bytes 7864320 | tf_op jit(solution)/shard_map/all_to_all | solution.py:23
  22.0 215.0 %all-gather.4.cloned.1.call-start = ((), (), s32[]{:S(2)}) async-start(), calls=%async_computation.1 | async-start | bytes 16711680 | tf_op jit(solution)/shard_map/all_gather | solution.py:43
  103.6 26.9 %copy-start.1 = (bf16[256,1920]{1,0:T(8,128)(2,1)S(1)}, bf16[256,1920]{1,0:T(8,128)(2,1)}, u32[]{:S(2)}) copy-start(bf16[256,1920]{1,0:T(8,128)(2,1)} %param.12) | copy-start | bytes 2949124
Sparse Core Ops, SparseCore 0:
  144.9 92.0 all-gather.3
